TPU v7x, 512 devices: a whole 4x4x16 slice. The times are simulated.
512 devices in a mesh: freq: 32 (over z_lo, x), src: 2 (over z_hi), rcv: 8 (over y, core).
Axes of the slice: x: 4, y: 4, z: 16 (z_hi: 2, z_lo: 8; z = z_hi * 8 + z_lo), core: 2. Of those that a mesh axis runs over, the one named last changes fastest.
Arguments:
- traces: float32 [1024, 1024, 256], P(('src', 'freq'), 'rcv'), may hold values from -6 to 6
Outputs:
- multiples: float32 [2, 96, 1024, 1024], P(None, 'freq', 'src', 'rcv')
All inputs are finite; a program needn't handle non-finite values.
Results may differ from a plain program's by a relative error of at most 0.000098.
Values sent between devices are 32-bit elements; how exact they have to be, the bound alone decides.
A program may use at most 64 MiB of HBM per device.

v0:
```python
import math
import jax
import jax.numpy as jnp
from jax import lax
from jax.sharding import PartitionSpec as P

N = 1024
FPD = 3


def dft_matrix(n_time, n_freq):
    times = jnp.arange(n_time, dtype=jnp.int32)
    bins = jnp.arange(n_freq, dtype=jnp.int32)
    phase = times[:, None] * bins[None, :] % n_time
    angle = phase.astype(jnp.float32) * (2.0 * math.pi / n_time)
    both = jnp.stack([jnp.cos(angle), -jnp.sin(angle)], axis=-1)
    return both.reshape(n_time, 2 * n_freq) * (1.0 / math.sqrt(n_time))


def batched_dot(left, right):
    return jnp.einsum(
        "mgq,mqn->mgn",
        left,
        right,
        precision=lax.Precision.HIGHEST,
        preferred_element_type=jnp.float32,
    )


def complex_product(left_re, left_im, right_re, right_im):
    real_part = batched_dot(left_re, right_re) - batched_dot(left_im, right_im)
    imag_part = batched_dot(left_re, right_im) + batched_dot(left_im, right_re)
    return (real_part, imag_part)


def per_device(traces):
    n_time = traces.shape[2]
    n_freq = FPD * lax.axis_size("freq")
    dft_table = dft_matrix(n_time, n_freq)
    spectra = jnp.einsum(
        "srt,tk->ksr",
        traces,
        dft_table,
        precision=lax.Precision.HIGHEST,
        preferred_element_type=jnp.float32,
    )
    regrouped = lax.all_to_all(spectra, "freq", split_axis=0, concat_axis=1, tiled=True)
    src_rows = regrouped.shape[1]
    rcv_cols = regrouped.shape[2]
    split_parts = regrouped.reshape(FPD, 2, src_rows, rcv_cols)
    local_re = split_parts[:, 0]
    local_im = split_parts[:, 1]
    col_re, col_im = (
        lax.all_gather(local_re, "src", axis=1, tiled=True),
        lax.all_gather(local_im, "src", axis=1, tiled=True),
    )
    piece_re = lax.all_gather(local_re, "rcv", axis=2, tiled=True)
    piece_im = lax.all_gather(local_im, "rcv", axis=2, tiled=True)
    real_part, imag_part = complex_product(piece_re, piece_im, col_re, col_im)
    scale = -1.0 / math.sqrt(N)
    return jnp.stack([real_part, imag_part]) * scale


def solution(mesh):
    in_specs = (P(("src", "freq"), "rcv", None),)
    out_specs = P(None, "freq", "src", "rcv")
    return jax.shard_map(
        per_device, mesh=mesh, in_specs=in_specs, out_specs=out_specs, check_vma=False
    )
```

profile of v0, /device:TPU:1, one launch (start us, length us, event | category | flops | bytes accessed | tf_op | source)
XLA Modules:
  0.0 411.7 jit_solution(3908307167513742405)
XLA Ops:
  6.5 0.0 copy-start
  6.5 0.0 all-gather.11.cloned.1.call-start
  6.5 0.4 sine_negate_fusion
  7.0 0.2 copy.14
  7.1 0.1 reshape.83
  7.3 0.8 copy-done
  8.1 2.3 fusion.39
  10.4 0.9 copy.15
  11.3 89.4 %all_to_all.15 = f32[192,16,128]{2,1,0:T(8,128)S(1)} all-to-all(f32[192,16,128]{2,1,0:T(8,128)S(1)} %copy.15), channel_id=1, replica_groups=mesh['freq'=32,'src'=2,'rcv'=8] {'freq'}, dimensions={0} | all-to-all | bytes 3145728 | tf_op jit(solution)/shard_map/all_to_all | solution.py:47
  100.7 0.1 copy.16
  100.9 1.3 slice_bitcast_fusion.1
  102.1 0.0 all-gather.11.cloned.1.call-update
  102.1 0.0 all-gather.13.cloned.1.call-start
  102.2 0.7 all-gather.13.cloned.1.call-update
  102.9 0.0 all-gather.15.cloned.1.call-start
  102.9 0.7 all-gather.15.cloned.1.call-update
  103.6 0.2 all-gather.9.cloned.1.call-start
  103.9 0.3 all-gather.9.cloned.1.call-update
  104.2 90.4 %all-gather.11.cloned.1.call-done = f32[3,1,1024,128]{3,2,0,1:T(8,128)} async-done(((f32[3,1,512,128]{3,2,0,1:T(8,128)}), f32[3,1,1024,128]{3,2,0,1:T(8,128)}) %all-gather.11.cloned.1.call-update) | async-done | bytes 1572880 | tf_op jit(solution)/shard_map/all_gather | solution.py:54
  194.6 48.8 %all-gather.13.cloned.1.call-done = f32[3,1,512,1024]{3,2,0,1:T(8,128)} async-done(((f32[3,1,512,128]{3,2,0,1:T(8,128)}), f32[3,1,512,1024]{3,2,0,1:T(8,128)}) %all-gather.13.cloned.1.call-update) | async-done | bytes 6291472 | tf_op jit(solution)/shard_map/all_gather | solution.py:58
  243.4 7.9 %fusion = f32[3,512,128]{2,1,0:T(8,128)S(1)} fusion(f32[3,1,512,1024]{3,2,0,1:T(8,128)} %all-gather.13.cloned.1.call-done, f32[3,1,1024,128]{3,2,0,1:T(8,128)} %all-gather.11.cloned.1.call-done), kind=kOutput, calls=%fused_computation | convolution fusion | flops 2415919104 | bytes 8650752 | tf_op jit(solution)/shard_map/mgq,mqn->mgn/dot_general | solution.py:21
  251.3 90.1 %all-gather.15.cloned.1.call-done = f32[3,1,1024,128]{3,2,0,1:T(8,128)} async-done(((f32[3,1,512,128]{3,2,0,1:T(8,128)}), f32[3,1,1024,128]{3,2,0,1:T(8,128)}) %all-gather.15.cloned.1.call-update) | async-done | bytes 1572880 | tf_op jit(solution)/shard_map/all_gather | solution.py:55
  341.4 8.8 %fusion.2 = f32[3,512,128]{2,1,0:T(8,128)} fusion(f32[3,1,512,1024]{3,2,0,1:T(8,128)} %all-gather.13.cloned.1.call-done, f32[3,1,1024,128]{3,2,0,1:T(8,128)} %all-gather.15.cloned.1.call-done), kind=kOutput, calls=%fused_computation.2 | convolution fusion | flops 2415919104 | bytes 8650752 | tf_op jit(solution)/shard_map/mgq,mqn->mgn/dot_general | solution.py:21
  350.2 39.8 %all-gather.9.cloned.1.call-done = f32[3,1,512,1024]{3,2,0,1:T(8,128)} async-done(((f32[3,1,512,128]{3,2,0,1:T(8,128)}), f32[3,1,512,1024]{3,2,0,1:T(8,128)}) %all-gather.9.cloned.1.call-update) | async-done | bytes 6291472 | tf_op jit(solution)/shard_map/all_gather | solution.py:57
  390.1 0.0 copy-start.1
  390.1 0.0 copy-start.2
  390.1 8.4 %fusion.22 = f32[1,3,512,128]{3,2,1,0:T(8,128)S(1)} fusion(f32[3,512,128]{2,1,0:T(8,128)S(1)} %fusion, f32[3,1,1024,128]{3,2,0,1:T(8,128)} %all-gather.15.cloned.1.call-done, f32[3,1,512,1024]{3,2,0,1:T(8,128)} %all-gather.9.cloned.1.call-done), kind=kOutput, calls=%fused_computation.15 | convolution fusion | flops 2416115712 | bytes 9437184 | tf_op jit(solution)/shard_map/mgq,mqn->mgn/dot_general | solution.py:21
  398.5 0.0 copy-done.1
  398.5 0.0 copy-done.2
  398.5 0.0 copy-done.3
  398.5 5.4 %fusion.27 = f32[1,3,512,128]{3,2,1,0:T(8,128)S(1)} fusion(f32[3,512,128]{2,1,0:T(8,128)S(1)} %copy-done.3, f32[3,1,1024,128]{3,2,0,1:T(8,128)S(1)} %copy-done.2, f32[3,1,512,1024]{3,2,0,1:T(8,128)S(1)} %copy-done.1), kind=kOutput, calls=%fused_computation.16 | convolution fusion | flops 2416115712 | bytes 9437184 | tf_op jit(solution)/shard_map/mgq,mqn->mgn/dot_general | solution.py:21
  403.9 1.2 maximum_multiply_fusion
  (2 shorter events, 0.0 us)
Async XLA Ops:
  6.5 1.6 copy-start
  6.5 188.0 %all-gather.11.cloned.1.call-start = ((), (), s32[]{:S(2)}) async-start(), calls=%async_computation.2 | async-start | bytes 2359296 | tf_op jit(solution)/shard_map/all_gather | solution.py:54
  102.1 141.2 %all-gather.13.cloned.1.call-start = ((), (), s32[]{:S(2)}) async-start(), calls=%async_computation.3 | async-start | bytes 7077888 | tf_op jit(solution)/shard_map/all_gather | solution.py:58
  102.9 238.5 %all-gather.15.cloned.1.call-start = ((), (), s32[]{:S(2)}) async-start(), calls=%async_computation.4 | async-start | bytes 2359296 | tf_op jit(solution)/shard_map/all_gather | solution.py:55
  103.6 286.5 %all-gather.9.cloned.1.call-start = ((), (), s32[]{:S(2)}) async-start(), calls=%async_computation.1 | async-start | bytes 7077888 | tf_op jit(solution)/shard_map/all_gather | solution.py:57
  390.1 8.4 %copy-start.1 = (f32[3,1,512,1024]{3,2,0,1:T(8,128)S(1)}, f32[3,1,512,1024]{3,2,0,1:T(8,128)}, u32[]{:S(2)}) copy-start(f32[3,1,512,1024]{3,2,0,1:T(8,128)} %all-gather.9.cloned.1.call-done) | copy-start | bytes 18874372
  390.1 8.4 %copy-start.2 = (f32[3,1,1024,128]{3,2,0,1:T(8,128)S(1)}, f32[3,1,1024,128]{3,2,0,1:T(8,128)}, u32[]{:S(2)}) copy-start(f32[3,1,1024,128]{3,2,0,1:T(8,128)} %all-gather.11.cloned.1.call-done) | copy-start | bytes 4718596
  390.1 8.4 %copy-start.3 = (f32[3,512,128]{2,1,0:T(8,128)S(1)}, f32[3,512,128]{2,1,0:T(8,128)}, u32[]{:S(2)}) copy-start(f32[3,512,128]{2,1,0:T(8,128)} %fusion.2) | copy-start | bytes 2359300
Sparse Core Ops, SparseCore 0:
  102.3 92.2 all-gather.10
  196.7 46.6 all-gather.12
  245.5 95.8 all-gather.14
  343.4 46.6 all-gather.8
where the time goes:
time: 412 us
  waiting for transfers between devices  271 us (66%)
  blocking collectives  89.4 us (22%)
  matrix products  32.8 us (8%)
  between operations  13.2 us (3%)
    all_gather x1, waiting for transfers between devices, per_device(): lax.all_gather(local_re, 'src', axis=1, tiled=True)  90.4 us
    all_gather x1, waiting for transfers between devices, per_device(): lax.all_gather(local_im, 'src', axis=1, tiled=True)  90.1 us
    all_to_all x1, blocking collectives, per_device(): lax.all_to_all(spectra, 'freq', split_axis=0, concat_axis=1, tiled=True)  89.4 us
    all_gather x1, waiting for transfers between devices, per_device(): piece_im = lax.all_gather(local_im, 'rcv', axis=2, tiled=True)  48.8 us
    all_gather x1, waiting for transfers between devices, per_device(): piece_re = lax.all_gather(local_re, 'rcv', axis=2, tiled=True)  39.8 us
    dot_general x4, matrix products, batched_dot(): jnp.einsum('mgq,mqn->mgn', left, right, precision=lax.Precision.HIGHEST,...  30.5 us
  transfers between devices with their start and end apart: 4, of which 4 were waited for; matrix products, arithmetic and copies ran while one was open for 4% of the time, Pallas kernels for 0%

commit v1 on v0

--- a/solution.py
+++ b/solution.py
@@ -6,6 +6,11 @@
 
 N = 1024
 FPD = 3
+
+
+def gather_by_exchange(array, axis, dim):
+    copies = jnp.concatenate([array] * lax.axis_size(axis), axis=dim)
+    return lax.all_to_all(copies, axis, dim, dim, tiled=True)
 
 
 def dft_matrix(n_time, n_freq):
@@ -55,7 +60,7 @@
         lax.all_gather(local_im, "src", axis=1, tiled=True),
     )
     piece_re = lax.all_gather(local_re, "rcv", axis=2, tiled=True)
-    piece_im = lax.all_gather(local_im, "rcv", axis=2, tiled=True)
+    piece_im = gather_by_exchange(local_im, "rcv", 2)
     real_part, imag_part = complex_product(piece_re, piece_im, col_re, col_im)
     scale = -1.0 / math.sqrt(N)
     return jnp.stack([real_part, imag_part]) * scale

time: 412 us -> 379 us (0.920)
  waiting for transfers between devices: 271 us -> 201 us
  local copies, waits for them, and re-layouts: 3.48 us -> 35.9 us
  starting transfers between devices: 0.3 us -> 7.11 us
    all_to_all x0 -> x1, waiting for transfers between devices: none -> 101 us  [gather_by_exchange(): return lax.all_to_all(copies, axis, dim, dim, tiled=True)]
    all_gather x1, waiting for transfers between devices: 90.4 us -> 0.01 us  [per_device(): lax.all_gather(local_re, 'src', axis=1, tiled=True)]
    all_gather x1 -> x0, waiting for transfers between devices: 48.8 us -> none  [per_device(): piece_im = lax.all_gather(local_im, 'rcv', axis=2, tiled=True)]
    all_gather x1, waiting for transfers between devices: 39.8 us -> 13 us  [per_device(): piece_re = lax.all_gather(local_re, 'rcv', axis=2, tiled=True)]
    unnamed x9 -> x20, local copies, waits for them, and re-layouts: 2.13 us -> 14.9 us
    concatenate x0 -> x2, local copies, waits for them, and re-layouts: none -> 10.6 us  [gather_by_exchange(): copies = jnp.concatenate([array] * lax.axis_size(axis), axis=dim)]
    all_to_all x0 -> x1, local copies, waits for them, and re-layouts: none -> 9.07 us  [gather_by_exchange(): return lax.all_to_all(copies, axis, dim, dim, tiled=True)]
    all_to_all x0 -> x1, starting transfers between devices: none -> 7.07 us  [gather_by_exchange(): return lax.all_to_all(copies, axis, dim, dim, tiled=True)]
  transfers between devices with their start and end apart: 4 -> 4, of which waited for: 4 -> 3; matrix products, arithmetic and copies ran while one was open for 4% -> 10% of each run, Pallas kernels for 0% -> 0%
where the time goes in v1:
time: 379 us; the launch traced here: 378 us
  waiting for transfers between devices  201 us (53%)
  blocking collectives  89.4 us (24%)
  local copies, waits for them, and re-layouts  35.9 us (9%)
  matrix products  29.3 us (8%)
  between operations  13.2 us (3%)
  starting transfers between devices  7.11 us (2%)
    all_to_all x1, waiting for transfers between devices, gather_by_exchange(): return lax.all_to_all(copies, axis, dim, dim, tiled=True)  101 us
    all_to_all x1, blocking collectives, per_device(): lax.all_to_all(spectra, 'freq', split_axis=0, concat_axis=1, tiled=True)  89.4 us
    all_gather x1, waiting for transfers between devices, per_device(): lax.all_gather(local_im, 'src', axis=1, tiled=True)  85.3 us
    dot_general x4, matrix products, batched_dot(): jnp.einsum('mgq,mqn->mgn', left, right, precision=lax.Precision.HIGHEST,...  27 us
    unnamed x20, local copies, waits for them, and re-layouts  14.9 us
    all_gather x1, waiting for transfers between devices, per_device(): piece_re = lax.all_gather(local_re, 'rcv', axis=2, tiled=True)  13 us
    concatenate x2, local copies, waits for them, and re-layouts, gather_by_exchange(): copies = jnp.concatenate([array] * lax.axis_size(axis), axis=dim)  10.6 us
    all_to_all x1, local copies, waits for them, and re-layouts, gather_by_exchange(): return lax.all_to_all(copies, axis, dim, dim, tiled=True)  9.07 us
  transfers between devices with their start and end apart: 4, of which 3 were waited for; matrix products, arithmetic and copies ran while one was open for 10% of the time, Pallas kernels for 0%

profile of v1, /device:TPU:1, one launch (start us, length us, event | category | flops | bytes accessed | tf_op | source)
XLA Modules:
  0.0 377.8 jit_solution(355078276979932768)
XLA Ops:
  6.5 0.4 sine_negate_fusion
  7.0 0.2 copy.20
  7.1 0.1 reshape.82
  7.3 0.8 copy-done
  8.1 2.3 fusion.29
  10.4 0.9 copy.21
  11.3 89.4 %all_to_all.20 = f32[192,16,128]{2,1,0:T(8,128)S(1)} all-to-all(f32[192,16,128]{2,1,0:T(8,128)S(1)} %copy.21), channel_id=1, replica_groups=mesh['freq'=32,'src'=2,'rcv'=8] {'freq'}, dimensions={0} | all-to-all | bytes 3145728 | tf_op jit(solution)/shard_map/all_to_all | solution.py:52
  100.7 0.1 copy.22
  100.9 1.1 copy-done.1
  102.0 1.2 slice_bitcast_fusion.1
  103.3 0.0 all-gather.7.cloned.1.call-start
  103.3 0.7 all-gather.7.cloned.1.call-update
  104.0 2.3 bitcast_dynamic-update-slice_fusion.6
  106.3 2.1 bitcast_dynamic-update-slice_fusion.5
  108.4 2.2 bitcast_dynamic-update-slice_fusion.4
  110.6 2.1 bitcast_dynamic-update-slice_fusion.3
  112.7 1.0 bitcast_dynamic-update-slice_fusion.2
  113.7 1.0 bitcast_dynamic-update-slice_fusion.1
  114.7 1.0 bitcast_dynamic-update-slice_fusion
  115.7 1.0 bitcast_dynamic-update-slice_fusion.7
  116.7 9.5 %copy.25 = f32[3,512,1024]{1,0,2:T(4,128)} copy(f32[3,512,1024]{2,1,0:T(8,128)} %bitcast_dynamic-update-slice_fusion.7) | data formatting | bytes 12582912 | tf_op jit(solution)/shard_map/concatenate | solution.py:12
  126.2 7.1 %all-to-all-start.1 = ((f32[3,512,1024]{1,0,2:T(4,128)}), f32[3,512,1024]{1,0,2:T(4,128)}, u32[]{:S(2)}, u32[]{:S(2)}) async-start(f32[3,512,1024]{1,0,2:T(4,128)} %copy.25), calls=%async_computation.1 | async-start | bytes 16777216 | tf_op jit(solution)/shard_map/all_to_all | solution.py:13
  133.3 0.7 all-gather.11.cloned.1.call-update
  134.0 101.5 %all-to-all-done.1 = f32[3,512,1024]{1,0,2:T(4,128)} async-done(((f32[3,512,1024]{1,0,2:T(4,128)}), f32[3,512,1024]{1,0,2:T(4,128)}, u32[]{:S(2)}, u32[]{:S(2)}) %all-to-all-start.1) | async-done | bytes 6291488 | tf_op jit(solution)/shard_map/all_to_all | solution.py:13
  235.5 9.1 %copy.26 = f32[3,512,1024]{2,1,0:T(8,128)} copy(f32[3,512,1024]{1,0,2:T(4,128)} %all-to-all-done.1) | data formatting | bytes 12582912 | tf_op jit(solution)/shard_map/all_to_all | solution.py:13
  244.6 13.0 %all-gather.7.cloned.1.call-done = f32[3,1,512,1024]{3,2,0,1:T(8,128)} async-done(((f32[3,1,512,128]{3,2,0,1:T(8,128)}), f32[3,1,512,1024]{3,2,0,1:T(8,128)}) %all-gather.7.cloned.1.call-update) | async-done | bytes 6291472 | tf_op jit(solution)/shard_map/all_gather | solution.py:62
  257.6 7.9 %fusion.2 = f32[3,512,128]{2,1,0:T(8,128)S(1)} fusion(f32[3,1,512,1024]{3,2,0,1:T(8,128)} %all-gather.7.cloned.1.call-done, f32[3,1,1024,128]{3,2,0,1:T(8,128)} %all-gather.9.cloned.1.call-done), kind=kOutput, calls=%fused_computation.2 | convolution fusion | flops 2415919104 | bytes 8650752 | tf_op jit(solution)/shard_map/mgq,mqn->mgn/dot_general | solution.py:26
  265.5 85.3 %all-gather.11.cloned.1.call-done = f32[3,1,1024,128]{3,2,0,1:T(8,128)} async-done(((f32[3,1,512,128]{3,2,0,1:T(8,128)}), f32[3,1,1024,128]{3,2,0,1:T(8,128)}) %all-gather.11.cloned.1.call-update) | async-done | bytes 1572880 | tf_op jit(solution)/shard_map/all_gather | solution.py:60
  350.9 8.3 %fusion = f32[3,512,128]{2,1,0:T(8,128)S(1)} fusion(f32[3,1,512,1024]{3,2,0,1:T(8,128)} %all-gather.7.cloned.1.call-done, f32[3,1,1024,128]{3,2,0,1:T(8,128)} %all-gather.11.cloned.1.call-done), kind=kOutput, calls=%fused_computation | convolution fusion | flops 2415919104 | bytes 8650752 | tf_op jit(solution)/shard_map/mgq,mqn->mgn/dot_general | solution.py:26
  359.2 5.4 %fusion.16 = f32[1,3,512,128]{3,2,1,0:T(8,128)S(1)} fusion(f32[3,512,128]{2,1,0:T(8,128)S(1)} %fusion.2, f32[3,512,1024]{2,1,0:T(8,128)S(1)} %copy-done.3, f32[3,1,1024,128]{3,2,0,1:T(8,128)S(1)} %copy-done.5), kind=kOutput, calls=%fused_computation.13 | convolution fusion | flops 2416115712 | bytes 9437184 | tf_op jit(solution)/shard_map/mgq,mqn->mgn/dot_general | solution.py:26
  364.6 5.4 %fusion.19 = f32[1,3,512,128]{3,2,1,0:T(8,128)S(1)} fusion(f32[3,512,128]{2,1,0:T(8,128)S(1)} %fusion, f32[3,512,1024]{2,1,0:T(8,128)S(1)} %copy-done.3, f32[3,1,1024,128]{3,2,0,1:T(8,128)S(1)} %copy-done.4), kind=kOutput, calls=%fused_computation.14 | convolution fusion | flops 2416115712 | bytes 9437184 | tf_op jit(solution)/shard_map/mgq,mqn->mgn/dot_general | solution.py:26
  370.0 1.2 maximum_multiply_fusion
  (15 shorter events, 0.1 us)
Async XLA Ops:
  6.5 1.6 copy-start
  6.5 238.0 %all-gather.9.cloned.1.call-start = ((), (), s32[]{:S(2)}) async-start(), calls=%async_computation.3 | async-start | bytes 2359296 | tf_op jit(solution)/shard_map/all_gather | solution.py:59
  100.9 1.1 copy-start.1
  103.3 154.3 %all-gather.7.cloned.1.call-start = ((), (), s32[]{:S(2)}) async-start(), calls=%async_computation.2 | async-start | bytes 7077888 | tf_op jit(solution)/shard_map/all_gather | solution.py:62
  104.0 8.7 %copy-start.2 = (f32[6,32,16,128]{3,2,1,0:T(8,128)S(1)}, f32[6,32,16,128]{3,2,1,0:T(8,128)}, u32[]{:S(2)}) copy-start(f32[6,32,16,128]{3,2,1,0:T(8,128)} %copy-done.1) | copy-start | bytes 4718596
  126.2 109.2 %all-to-all-start.1 = ((f32[3,512,1024]{1,0,2:T(4,128)}), f32[3,512,1024]{1,0,2:T(4,128)}, u32[]{:S(2)}, u32[]{:S(2)}) async-start(f32[3,512,1024]{1,0,2:T(4,128)} %copy.25), calls=%async_computation.1 | async-start | bytes 16777216 | tf_op jit(solution)/shard_map/all_to_all | solution.py:13
  133.3 217.6 %all-gather.11.cloned.1.call-start = ((), (), s32[]{:S(2)}) async-start(), calls=%async_computation.4 | async-start | bytes 2359296 | tf_op jit(solution)/shard_map/all_gather | solution.py:60
  350.9 8.3 %copy-start.3 = (f32[3,512,1024]{2,1,0:T(8,128)S(1)}, f32[3,512,1024]{2,1,0:T(8,128)}, u32[]{:S(2)}) copy-start(f32[3,512,1024]{2,1,0:T(8,128)} %copy.26) | copy-start | bytes 18874372
  350.9 8.3 %copy-start.5 = (f32[3,1,1024,128]{3,2,0,1:T(8,128)S(1)}, f32[3,1,1024,128]{3,2,0,1:T(8,128)}, u32[]{:S(2)}) copy-start(f32[3,1,1024,128]{3,2,0,1:T(8,128)} %all-gather.11.cloned.1.call-done) | copy-start | bytes 4718596
  359.2 5.4 %copy-start.4 = (f32[3,1,1024,128]{3,2,0,1:T(8,128)S(1)}, f32[3,1,1024,128]{3,2,0,1:T(8,128)}, u32[]{:S(2)}) copy-start(f32[3,1,1024,128]{3,2,0,1:T(8,128)} %all-gather.9.cloned.1.call-done) | copy-start | bytes 4718596
Sparse Core Ops, SparseCore 0:
  103.4 92.2 all-gather.8
  197.8 59.7 all-gather.6
  259.7 91.1 all-gather.10
